TPU v7x, 32 devices: a whole 2x2x4 slice. The times are simulated.
32 devices in a mesh: row: 8 (over y, x, core), col: 4 (over z).
Axes of the slice: x: 2, y: 2, z: 4, core: 2. Of those that a mesh axis runs over, the one named last changes fastest.
Arguments:
- panel_tiles: float32 [16384, 1024], P('row', 'col'), may hold values from -48 to 48
- left_u: bfloat16 [16384, 6144], P('row', 'col'), may hold values from -8 to 8
- earlier_right_factors: bfloat16 [16384, 6144], P('row', 'col'), may hold values from -0.25 to 0.25
- tile_global_index: int32 [16], replicated, may hold values from 0 to 15, as said below
Outputs:
- panel_factor: float32 [16384, 1024], P('row', 'col')
Inputs may be any that keep to these rules, and one draw needn't show every extreme that they name: `tile_global_index`: A permutation; slot pivot, the one numbered 0, holds the diagonal tile.
All inputs are finite; a program needn't handle non-finite values.
Results may differ from a plain program's by a relative error of at most 0.00053.
Values may be sent and summed in bfloat16 or wider, within the bound.
A program may use at most 128 MiB of HBM per device.

v0:
```python
import jax
import jax.numpy as jnp
from jax import lax
from jax.sharding import PartitionSpec as P

TILE = 1024
RANK = 256
TILE_DEV = 2
COL_DEV = 6


def from_root(value, axis, source):
    kept = jnp.where(lax.axis_index(axis) == source, value, 0).astype(value.dtype)
    return lax.psum(kept, axis)


def local(panel_tiles, left_u, earlier_right_factors, tile_global_index):
    tile_count = tile_global_index.shape[0]
    pivot_position = jnp.sum(
        jnp.where(tile_global_index == 0, jnp.arange(tile_count, dtype=jnp.int32), 0)
    )
    owner_row = pivot_position // TILE_DEV
    local_slot = pivot_position % TILE_DEV
    my_row = lax.axis_index("row")
    my_col = lax.axis_index("col")
    col_width = panel_tiles.shape[1]
    pivot_left = lax.dynamic_slice_in_dim(left_u, local_slot * TILE, TILE, 0)
    pivot_right = lax.dynamic_slice_in_dim(earlier_right_factors, local_slot * TILE, TILE, 0)
    pivot_left, pivot_right = (
        from_root(pivot_left, "row", owner_row),
        from_root(pivot_right, "row", owner_row),
    )
    left_blocks = left_u.reshape(TILE_DEV, TILE, COL_DEV, RANK)
    right_blocks = earlier_right_factors.reshape(TILE_DEV, TILE, COL_DEV, RANK)
    pivot_triple = pivot_right.reshape(TILE, COL_DEV, RANK)
    inner_small = jnp.einsum(
        "tbjr,bjs->tjrs", right_blocks, pivot_triple, preferred_element_type=jnp.float32
    ).astype(jnp.bfloat16)
    left_small = jnp.einsum(
        "tbjr,tjrs->tbjs", left_blocks, inner_small, preferred_element_type=jnp.float32
    ).astype(jnp.bfloat16)
    update_terms = jnp.einsum(
        "nk,mk->nm",
        left_small.reshape(TILE_DEV * TILE, COL_DEV * RANK),
        pivot_left,
        preferred_element_type=jnp.float32,
    )
    placed = lax.dynamic_update_slice_in_dim(
        jnp.zeros_like(update_terms), panel_tiles, my_col * col_width, 1
    )
    updated_tiles = lax.psum(placed - update_terms, "col")
    diagonal = lax.dynamic_slice_in_dim(updated_tiles, local_slot * TILE, TILE, 0)
    identity = jnp.eye(TILE, dtype=jnp.float32)
    cholesky_factor = jnp.linalg.cholesky(diagonal)
    inverted_factor = lax.linalg.triangular_solve(
        cholesky_factor, identity, left_side=True, lower=True
    )
    rows_inv = lax.dynamic_slice_in_dim(inverted_factor, my_col * col_width, col_width, 0)
    rows_inv = from_root(rows_inv, "row", owner_row)
    solved_rows = lax.dot_general(
        updated_tiles,
        rows_inv,
        (((1,), (1,)), ((), ())),
        precision=lax.Precision.HIGHEST,
        preferred_element_type=jnp.float32,
    )
    factor_cols = lax.dynamic_slice_in_dim(cholesky_factor, my_col * col_width, col_width, 1)
    row_tiles = jnp.arange(TILE_DEV * TILE, dtype=jnp.int32) // TILE
    chosen_rows = jnp.logical_and(my_row == owner_row, row_tiles == local_slot)
    return jnp.where(chosen_rows[:, None], jnp.tile(factor_cols, (TILE_DEV, 1)), solved_rows)


def solution(mesh):
    in_specs = (P("row", "col"), P("row", "col"), P("row", "col"), P())
    out_specs = P("row", "col")
    return jax.shard_map(local, mesh=mesh, in_specs=in_specs, out_specs=out_specs, check_vma=False)
```

profile of v0, /device:TPU:0, one launch (start us, length us, event | category | flops | bytes accessed | tf_op | source)
XLA Modules:
  0.0 900.8 jit_solution(1738015696041004447)
XLA Ops:
  10.7 5.9 constant_dynamic-slice_fusion.3
  16.6 3.2 copy.24
  19.8 4.7 copy.25
  24.5 2.0 broadcast_select_fusion.1
  27.5 2.0 broadcast_select_fusion
  29.6 13.5 %reshape.127 = bf16[2,1024,6,256]{3,2,1,0:T(8,128)(2,1)} reshape(bf16[2048,1536]{1,0:T(8,128)(2,1)} %param.5) | data formatting | bytes 12582912 | tf_op jit(solution)/shard_map/reshape | solution.py:33
  43.1 13.4 %reshape.126 = bf16[2,1024,6,256]{3,2,1,0:T(8,128)(2,1)} reshape(bf16[2048,1536]{1,0:T(8,128)(2,1)} %param.6) | data formatting | bytes 12582912 | tf_op jit(solution)/shard_map/reshape | solution.py:34
  56.5 1.9 copy.9
  58.5 4.3 broadcast_in_dim.26
  64.3 72.1 %all-reduce.10.cloned.1.call-done = (bf16[1024,6,256]{0,2,1:T(8,128)(2,1)}, bf16[1024,1536]{0,1:T(8,128)(2,1)}) async-done(((bf16[1024,6,256]{0,2,1:T(8,128)(2,1)}, bf16[1024,1536]{0,1:T(8,128)(2,1)}), (bf16[1024,6,256]{0,2,1:T(8,128)(2,1)}, bf16[1024,1536]{0,1:T(8,128)(2,1)})) %all-reduce.10.cloned.1.call-update) | async-done | bytes 6291472 | tf_op jit(solution)/shard_map/psum | solution.py:14
  136.3 16.6 %convert_bitcast_fusion = bf16[2,1024,6,256]{1,3,2,0:T(8,128)(2,1)} fusion(bf16[2,1024,6,256]{3,2,1,0:T(8,128)(2,1)} %reshape.127, bf16[2,1024,6,256]{3,2,1,0:T(8,128)(2,1)} %reshape.126, bf16[1024,6,256]{0,2,1:T(8,128)(2,1)} %get-tuple-element.21), kind=kOutput, calls=%fused_computation.6 | convolution fusion | flops 3225157632 | bytes 22020096 | tf_op jit(solution)/shard_map/tbjr,tjrs->tbjs/dot_general | solution.py:39
  152.9 11.9 %copy.14 = bf16[2,1024,6,256]{1,0,3,2:T(2,128)(2,1)S(1)} copy(bf16[2,1024,6,256]{1,3,2,0:T(8,128)(2,1)} %convert_bitcast_fusion) | data formatting | bytes 12582912 | tf_op jit(solution)/shard_map/convert_element_type | solution.py:41
  164.9 2.7 copy.26
  167.5 11.9 %convolution_subtract_fusion = f32[2048,1024]{0,1:T(8,128)} fusion(f32[2048,1024]{0,1:T(8,128)} %constant_dynamic-update-slice_fusion.26, bf16[2048,1536]{0,1:T(8,128)(2,1)S(1)} %bitcast.129, bf16[1024,1536]{0,1:T(8,128)(2,1)S(1)} %copy-done.3), kind=kOutput, calls=%fused_computation.13 | convolution fusion | flops 6444548096 | bytes 26214400 | tf_op jit(solution)/shard_map/nk,mk->nm/dot_general | solution.py:42
  179.8 2.4 fusion.43
  182.3 288.3 %all-reduce.6.cloned.1.call-done = f32[2048,1024]{0,1:T(8,128)} async-done(((f32[2048,1024]{0,1:T(8,128)}), f32[2048,1024]{0,1:T(8,128)}) %all-reduce.6.cloned.1.call-update) | async-done | bytes 8388624 | tf_op jit(solution)/shard_map/psum | solution.py:51
  470.5 4.7 constant_dynamic-slice_fusion.2
  475.3 5.4 copy.17
  480.6 4.4 fusion.4
  485.1 2.0 copy-done.2
  487.1 11.7 %cholesky.223 = f32[128,128]{1,0:T(8,128)S(1)} custom-call(f32[128,128]{1,0:T(8,128)S(1)} %cholesky.580), custom_call_target="Cholesky" | custom-call | tf_op jit(solution)/shard_map/jit(cholesky)/cholesky | solution.py:54
  498.8 2.5 cholesky.255
  501.3 9.8 %custom-call.62 = f32[1,128,128]{1,2,0:T(8,128)S(1)} custom-call(f32[1,128,128]{2,1,0:T(8,128)S(1)} %get-tuple-element.73), custom_call_target="InvertDiagBlocksLowerTriangular" | custom-call | tf_op jit(solution)/shard_map/jit(cholesky)/cholesky | solution.py:54
  511.1 2.4 constant_dynamic-update-slice_fusion.25
  513.5 1.5 convolution_subtract_fusion.6
  515.0 11.9 %cholesky.244 = f32[128,128]{1,0:T(8,128)S(1)} custom-call(f32[128,128]{1,0:T(8,128)S(1)} %cholesky.584), custom_call_target="Cholesky" | custom-call | tf_op jit(solution)/shard_map/jit(cholesky)/cholesky | solution.py:54
  527.5 9.8 %custom-call.63 = f32[1,128,128]{1,2,0:T(8,128)S(1)} custom-call(f32[1,128,128]{2,1,0:T(8,128)S(1)} %get-tuple-element.70), custom_call_target="InvertDiagBlocksLowerTriangular" | custom-call | tf_op jit(solution)/shard_map/jit(cholesky)/cholesky | solution.py:54
  538.6 2.1 convolution_subtract_fusion.7
  540.7 11.7 %cholesky.468 = f32[128,128]{1,0:T(8,128)S(1)} custom-call(f32[128,128]{1,0:T(8,128)S(1)} %cholesky.589), custom_call_target="Cholesky" | custom-call | tf_op jit(solution)/shard_map/jit(cholesky)/cholesky | solution.py:54
  553.1 9.8 %custom-call.64 = f32[1,128,128]{1,2,0:T(8,128)S(1)} custom-call(f32[1,128,128]{2,1,0:T(8,128)S(1)} %get-tuple-element.67), custom_call_target="InvertDiagBlocksLowerTriangular" | custom-call | tf_op jit(solution)/shard_map/jit(cholesky)/cholesky | solution.py:54
  564.1 2.3 convolution_subtract_fusion.8
  566.4 11.9 %cholesky.487 = f32[128,128]{1,0:T(8,128)S(1)} custom-call(f32[128,128]{1,0:T(8,128)S(1)} %cholesky.594), custom_call_target="Cholesky" | custom-call | tf_op jit(solution)/shard_map/jit(cholesky)/cholesky | solution.py:54
  579.0 9.8 %custom-call.65 = f32[1,128,128]{1,2,0:T(8,128)S(1)} custom-call(f32[1,128,128]{2,1,0:T(8,128)S(1)} %get-tuple-element.64), custom_call_target="InvertDiagBlocksLowerTriangular" | custom-call | tf_op jit(solution)/shard_map/jit(cholesky)/cholesky | solution.py:54
  589.9 2.3 convolution_subtract_fusion.9
  592.3 11.7 %cholesky.506 = f32[128,128]{1,0:T(8,128)S(1)} custom-call(f32[128,128]{1,0:T(8,128)S(1)} %cholesky.599), custom_call_target="Cholesky" | custom-call | tf_op jit(solution)/shard_map/jit(cholesky)/cholesky | solution.py:54
  604.6 10.2 %custom-call.66 = f32[1,128,128]{1,2,0:T(8,128)S(1)} custom-call(f32[1,128,128]{2,1,0:T(8,128)S(1)} %get-tuple-element.61), custom_call_target="InvertDiagBlocksLowerTriangular" | custom-call | tf_op jit(solution)/shard_map/jit(cholesky)/cholesky | solution.py:54
  615.8 2.3 convolution_subtract_fusion.10
  618.1 11.7 %cholesky.526 = f32[128,128]{1,0:T(8,128)S(1)} custom-call(f32[128,128]{1,0:T(8,128)S(1)} %cholesky.604), custom_call_target="Cholesky" | custom-call | tf_op jit(solution)/shard_map/jit(cholesky)/cholesky | solution.py:54
  630.5 9.8 %custom-call.67 = f32[1,128,128]{1,2,0:T(8,128)S(1)} custom-call(f32[1,128,128]{2,1,0:T(8,128)S(1)} %get-tuple-element.58), custom_call_target="InvertDiagBlocksLowerTriangular" | custom-call | tf_op jit(solution)/shard_map/jit(cholesky)/cholesky | solution.py:54
  641.2 2.0 convolution_subtract_fusion.11
  643.3 11.7 %cholesky.546 = f32[128,128]{1,0:T(8,128)S(1)} custom-call(f32[128,128]{1,0:T(8,128)S(1)} %cholesky.609), custom_call_target="Cholesky" | custom-call | tf_op jit(solution)/shard_map/jit(cholesky)/cholesky | solution.py:54
  655.6 9.8 %custom-call.68 = f32[1,128,128]{1,2,0:T(8,128)S(1)} custom-call(f32[1,128,128]{2,1,0:T(8,128)S(1)} %get-tuple-element.55), custom_call_target="InvertDiagBlocksLowerTriangular" | custom-call | tf_op jit(solution)/shard_map/jit(cholesky)/cholesky | solution.py:54
  666.3 1.8 convolution_subtract_fusion.12
  668.1 11.7 %cholesky.564 = f32[128,128]{1,0:T(8,128)S(1)} custom-call(f32[128,128]{1,0:T(8,128)S(1)} %convolution_subtract_fusion.12), custom_call_target="Cholesky" | custom-call | tf_op jit(solution)/shard_map/jit(cholesky)/cholesky | solution.py:54
  690.5 4.4 fusion.5
  694.9 22.9 %while.1 = (s32[]{:T(128)}, f32[1024,1024]{1,0:T(8,128)}, s32[8,2]{0,1:T(2,128)S(1)}, f32[8,128,128]{2,1,0:T(8,128)S(1)}, s32[]{:T(128)}) while((s32[]{:T(128)}, f32[1024,1024]{1,0:T(8,128)}, s32[8,2]{0,1:T(2,128)S(1)}, f32[8,128,128]{2,1,0:T(8,128)S(1)}, s32[]{:T(128)}) %tuple.58), condition=%wide.while_cond, body=%wide.while_body.sunk | while | flops 2 | bytes 131189 | solution.py:55
  695.6 2.2 bitcast_dynamic-update-slice_fusion.2
  698.4 2.2 bitcast_dynamic-update-slice_fusion.2
  701.3 2.2 bitcast_dynamic-update-slice_fusion.2
  704.2 2.2 bitcast_dynamic-update-slice_fusion.2
  707.1 2.2 bitcast_dynamic-update-slice_fusion.2
  709.9 2.2 bitcast_dynamic-update-slice_fusion.2
  712.8 2.2 bitcast_dynamic-update-slice_fusion.2
  715.7 2.2 bitcast_dynamic-update-slice_fusion.2
  717.8 78.8 %custom-call.69 = f32[8,128,128]{1,2,0:T(8,128)S(1)} custom-call(f32[8,128,128]{2,1,0:T(8,128)S(1)} %get-tuple-element.12), custom_call_target="InvertDiagBlocksLowerTriangular" | custom-call | tf_op jit(solution)/shard_map/triangular_solve | solution.py:55
  797.2 1.9 convolution_subtract_fusion.5
  799.9 1.6 convolution_subtract_fusion.1
  802.3 2.0 fusion.37
  805.1 2.2 fusion.40
  808.0 2.6 convolution_subtract_fusion.3
  811.4 2.8 convolution_subtract_fusion.2
  814.8 3.5 convolution_subtract_fusion.4
  821.4 55.3 %all-reduce.8.cloned.1.call-done = f32[256,1024]{1,0:T(8,128)} async-done(((f32[256,1024]{1,0:T(8,128)}), f32[256,1024]{1,0:T(8,128)}) %all-reduce.8.cloned.1.call-update) | async-done | bytes 1048592 | tf_op jit(solution)/shard_map/psum | solution.py:14
  876.9 17.0 %convolution_select_fusion = f32[2048,256]{1,0:T(8,128)} fusion(f32[2048,256]{1,0:T(8,128)S(1)} %bitcast.127, f32[2048,1024]{0,1:T(8,128)} %all-reduce.6.cloned.1.call-done, f32[256,1024]{1,0:T(8,128)} %all-reduce.8.cloned.1.call-done, pred[2048]{0:T(1024)(128)(4,1)S(1)} %fusion.93), kind=kOutput, calls=%fused_computation.17 | convolution fusion | flops 6442975232 | bytes 13633536 | tf_op jit(solution)/shard_map/dot_general | solution.py:60
  (76 shorter events, 33.4 us)
Async XLA Ops:
  6.5 129.8 %all-reduce.10.cloned.1.call-start = ((), (), s32[]{:S(2)}) async-start(), calls=%async_computation.2 | async-start | bytes 12582912 | tf_op jit(solution)/shard_map/psum | solution.py:14
  24.5 3.0 copy-start.1
  29.5 441.0 %all-reduce.6.cloned.1.call-start = ((), (), s32[]{:S(2)}) async-start(), calls=%async_computation | async-start | bytes 16777216 | tf_op jit(solution)/shard_map/psum | solution.py:51
  164.9 2.7 copy-start.3
  179.4 697.3 %all-reduce.8.cloned.1.call-start = ((), (), s32[]{:S(2)}) async-start(), calls=%async_computation.1 | async-start | bytes 2097152 | tf_op jit(solution)/shard_map/psum | solution.py:14
  485.1 2.0 copy-start.2
  796.7 3.2 copy-start
Sparse Core Ops, SparseCore 0:
  29.6 106.6 all-reduce.9
  179.6 290.9 all-reduce.5
  820.2 56.4 all-reduce.7
where the time goes:
time: 912 us; the launch traced here: 901 us
  waiting for transfers between devices  416 us (46%)
  other arithmetic  270 us (30%)
  local copies, waits for them, and re-layouts  103 us (11%)
  matrix products  90.7 us (10%)
  between operations  21.6 us (2%)
    psum x1, waiting for transfers between devices, local(): updated_tiles = lax.psum(placed - update_terms, 'col')  288 us
    another operation x31, other arithmetic, local(): cholesky_factor = jnp.linalg.cholesky(diagonal)  173 us
    psum x2, waiting for transfers between devices, from_root(): return lax.psum(kept, axis)  127 us
    another operation x3, other arithmetic, local(): lax.linalg.triangular_solve(cholesky_factor, identity, left_side=True, lo...  83.2 us
    another operation x14, matrix products, local(): cholesky_factor = jnp.linalg.cholesky(diagonal)  23.1 us
    another operation x24, local copies, waits for them, and re-layouts  22.7 us
    another operation x15, matrix products, local(): lax.linalg.triangular_solve(cholesky_factor, identity, left_side=True, lo...  22.2 us
  transfers between devices with their start and end apart: 3, of which 3 were waited for; matrix products, arithmetic and copies ran while one was open for 4% of the time, Pallas kernels for 0%

commit v1 on v0

--- a/solution.py
+++ b/solution.py
@@ -11,7 +11,7 @@
 
 def from_root(value, axis, source):
     kept = jnp.where(lax.axis_index(axis) == source, value, 0).astype(value.dtype)
-    return lax.psum(kept, axis)
+    return jnp.sum(lax.all_gather(kept, axis), axis=0)
 
 
 def local(panel_tiles, left_u, earlier_right_factors, tile_global_index):

time: 912 us -> 1060 us (1.16)
  waiting for transfers between devices: 416 us -> 541 us
  other arithmetic: 270 us -> 308 us
  local copies, waits for them, and re-layouts: 103 us -> 92 us
    all_gather x0 -> x3, waiting for transfers between devices: none -> 253 us  [from_root(): return jnp.sum(lax.all_gather(kept, axis), axis=0)]
    psum x2 -> x0, waiting for transfers between devices: 127 us -> none  [from_root(): return lax.psum(kept, axis)]
    reduce_sum x0 -> x3, other arithmetic: none -> 34.7 us  [from_root(): return jnp.sum(lax.all_gather(kept, axis), axis=0)]
    another operation x31 -> x30, other arithmetic: 173 us -> 172 us  [local(): cholesky_factor = jnp.linalg.cholesky(diagonal)]
  transfers between devices with their start and end apart: 3 -> 4, of which waited for: 3 -> 4; matrix products, arithmetic and copies ran while one was open for 4% -> 6% of each run, Pallas kernels for 0% -> 0%
where the time goes in v1:
time: 1060 us; the launch traced here: 1050 us
  waiting for transfers between devices  541 us (51%)
  other arithmetic  308 us (29%)
  local copies, waits for them, and re-layouts  92 us (9%)
  matrix products  89.5 us (8%)
  between operations  21.6 us (2%)
    psum x1, waiting for transfers between devices, local(): updated_tiles = lax.psum(placed - update_terms, 'col')  288 us
    all_gather x3, waiting for transfers between devices, from_root(): return jnp.sum(lax.all_gather(kept, axis), axis=0)  253 us
    another operation x30, other arithmetic, local(): cholesky_factor = jnp.linalg.cholesky(diagonal)  172 us
    another operation x3, other arithmetic, local(): lax.linalg.triangular_solve(cholesky_factor, identity, left_side=True, lo...  83.3 us
    reduce_sum x3, other arithmetic, from_root(): return jnp.sum(lax.all_gather(kept, axis), axis=0)  34.7 us
    another operation x24, local copies, waits for them, and re-layouts  23.4 us
    another operation x14, matrix products, local(): cholesky_factor = jnp.linalg.cholesky(diagonal)  23.1 us
    another operation x15, matrix products, local(): lax.linalg.triangular_solve(cholesky_factor, identity, left_side=True, lo...  22.2 us
  transfers between devices with their start and end apart: 4, of which 4 were waited for; matrix products, arithmetic and copies ran while one was open for 6% of the time, Pallas kernels for 0%

profile of v1, /device:TPU:0, one launch (start us, length us, event | category | flops | bytes accessed | tf_op | source)
XLA Modules:
  0.0 1052.3 jit_solution(16338224078925837357)
XLA Ops:
  10.7 4.1 dynamic-slice_select_fusion
  14.9 4.2 dynamic-slice_select_fusion.1
  19.2 13.7 %reshape.130 = bf16[2,1024,6,256]{3,2,1,0:T(8,128)(2,1)} reshape(bf16[2048,1536]{1,0:T(8,128)(2,1)} %param.5) | data formatting | bytes 12582912 | tf_op jit(solution)/shard_map/reshape | solution.py:33
  32.9 13.3 %reshape.129 = bf16[2,1024,6,256]{3,2,1,0:T(8,128)(2,1)} reshape(bf16[2048,1536]{1,0:T(8,128)(2,1)} %param.6) | data formatting | bytes 12582912 | tf_op jit(solution)/shard_map/reshape | solution.py:34
  46.2 1.9 copy.16
  48.1 4.2 broadcast_in_dim.26
  53.8 89.1 %all-gather.9.cloned.1.call-done = bf16[8192,1536]{1,0:T(8,128)(2,1)} async-done(((bf16[1024,1536]{1,0:T(8,128)(2,1)}), bf16[8192,1536]{1,0:T(8,128)(2,1)}) %all-gather.9.cloned.1.call-update) | async-done | bytes 25165840 | tf_op jit(solution)/shard_map/all_gather | solution.py:14
  142.9 16.5 %reduce_sum.44 = bf16[1024,1536]{1,0:T(8,128)(2,1)} reduce(bf16[8,1024,1536]{2,1,0:T(8,128)(2,1)} %bitcast.124, bf16[]{:T(256)} %constant.325.clone.1), dimensions={0}, to_apply=%region_2.3 | reduce | flops 11010048 | bytes 28311554 | tf_op jit(solution)/shard_map/reduce_sum | solution.py:14
  159.4 110.6 %all-gather.7.cloned.1.call-done = bf16[8192,1536]{1,0:T(8,128)(2,1)} async-done(((bf16[1024,1536]{1,0:T(8,128)(2,1)}), bf16[8192,1536]{1,0:T(8,128)(2,1)}) %all-gather.7.cloned.1.call-update) | async-done | bytes 25165840 | tf_op jit(solution)/shard_map/all_gather | solution.py:14
  270.0 13.8 %reduce_sum.43 = bf16[1024,1536]{1,0:T(8,128)(2,1)S(1)} reduce(bf16[8,1024,1536]{2,1,0:T(8,128)(2,1)} %bitcast.125, bf16[]{:T(256)} %constant.325.clone.1), dimensions={0}, to_apply=%region_1.2 | reduce | flops 11010048 | bytes 28311554 | tf_op jit(solution)/shard_map/reduce_sum | solution.py:14
  283.8 3.0 copy.17
  286.8 16.6 %convert_bitcast_fusion = bf16[2,1024,6,256]{1,3,2,0:T(8,128)(2,1)} fusion(bf16[2,1024,6,256]{3,2,1,0:T(8,128)(2,1)} %reshape.130, bf16[1024,6,256,1]{0,2,1,3:T(8,128)(2,1)} %bitcast.129, bf16[2,1024,6,256]{3,2,1,0:T(8,128)(2,1)} %reshape.129), kind=kOutput, calls=%fused_computation.6 | convolution fusion | flops 3225157632 | bytes 22020096 | tf_op jit(solution)/shard_map/tbjr,tjrs->tbjs/dot_general | solution.py:39
  303.4 12.3 %copy.22 = bf16[2,1024,6,256]{1,0,3,2:T(2,128)(2,1)S(1)} copy(bf16[2,1024,6,256]{1,3,2,0:T(8,128)(2,1)} %convert_bitcast_fusion) | data formatting | bytes 12582912 | tf_op jit(solution)/shard_map/convert_element_type | solution.py:41
  315.7 2.7 copy.30
  318.3 11.0 %convolution_subtract_fusion = f32[2048,1024]{0,1:T(8,128)} fusion(f32[2048,1024]{0,1:T(8,128)} %constant_dynamic-update-slice_fusion.26, bf16[1024,1536]{1,0:T(8,128)(2,1)S(1)} %copy-done.2, bf16[2048,1536]{0,1:T(8,128)(2,1)S(1)} %bitcast.128), kind=kOutput, calls=%fused_computation.13 | convolution fusion | flops 6444548096 | bytes 26214400 | tf_op jit(solution)/shard_map/nk,mk->nm/dot_general | solution.py:42
  329.8 2.4 fusion.36
  332.2 288.1 %all-reduce.3.cloned.1.call-done = f32[2048,1024]{0,1:T(8,128)} async-done(((f32[2048,1024]{0,1:T(8,128)}), f32[2048,1024]{0,1:T(8,128)}) %all-reduce.3.cloned.1.call-update) | async-done | bytes 8388624 | tf_op jit(solution)/shard_map/psum | solution.py:51
  620.3 4.7 constant_dynamic-slice_fusion.2
  625.1 5.4 copy.24
  630.5 4.4 fusion.4
  634.9 2.0 copy-done.1
  636.9 11.7 %cholesky.223 = f32[128,128]{1,0:T(8,128)S(1)} custom-call(f32[128,128]{1,0:T(8,128)S(1)} %cholesky.580), custom_call_target="Cholesky" | custom-call | tf_op jit(solution)/shard_map/jit(cholesky)/cholesky | solution.py:54
  648.6 2.5 cholesky.255
  651.1 9.8 custom-call.62
  660.9 2.4 constant_dynamic-update-slice_fusion.25
  664.9 11.9 %cholesky.244 = f32[128,128]{1,0:T(8,128)S(1)} custom-call(f32[128,128]{1,0:T(8,128)S(1)} %cholesky.584), custom_call_target="Cholesky" | custom-call | tf_op jit(solution)/shard_map/jit(cholesky)/cholesky | solution.py:54
  677.4 9.8 custom-call.63
  688.5 2.1 convolution_subtract_fusion.7
  690.6 11.7 %cholesky.468 = f32[128,128]{1,0:T(8,128)S(1)} custom-call(f32[128,128]{1,0:T(8,128)S(1)} %cholesky.589), custom_call_target="Cholesky" | custom-call | tf_op jit(solution)/shard_map/jit(cholesky)/cholesky | solution.py:54
  702.9 9.8 custom-call.64
  713.9 2.3 convolution_subtract_fusion.8
  716.3 11.9 %cholesky.487 = f32[128,128]{1,0:T(8,128)S(1)} custom-call(f32[128,128]{1,0:T(8,128)S(1)} %cholesky.594), custom_call_target="Cholesky" | custom-call | tf_op jit(solution)/shard_map/jit(cholesky)/cholesky | solution.py:54
  728.9 9.8 custom-call.65
  739.8 2.3 convolution_subtract_fusion.9
  742.1 11.7 %cholesky.506 = f32[128,128]{1,0:T(8,128)S(1)} custom-call(f32[128,128]{1,0:T(8,128)S(1)} %cholesky.599), custom_call_target="Cholesky" | custom-call | tf_op jit(solution)/shard_map/jit(cholesky)/cholesky | solution.py:54
  754.5 10.2 custom-call.66
  765.7 2.3 convolution_subtract_fusion.10
  768.0 11.7 %cholesky.526 = f32[128,128]{1,0:T(8,128)S(1)} custom-call(f32[128,128]{1,0:T(8,128)S(1)} %cholesky.604), custom_call_target="Cholesky" | custom-call | tf_op jit(solution)/shard_map/jit(cholesky)/cholesky | solution.py:54
  780.3 9.8 custom-call.67
  791.1 2.0 convolution_subtract_fusion.11
  793.1 11.7 %cholesky.546 = f32[128,128]{1,0:T(8,128)S(1)} custom-call(f32[128,128]{1,0:T(8,128)S(1)} %cholesky.609), custom_call_target="Cholesky" | custom-call | tf_op jit(solution)/shard_map/jit(cholesky)/cholesky | solution.py:54
  805.5 9.8 custom-call.68
  816.1 1.8 convolution_subtract_fusion.12
  817.9 11.7 %cholesky.564 = f32[128,128]{1,0:T(8,128)S(1)} custom-call(f32[128,128]{1,0:T(8,128)S(1)} %convolution_subtract_fusion.12), custom_call_target="Cholesky" | custom-call | tf_op jit(solution)/shard_map/jit(cholesky)/cholesky | solution.py:54
  839.7 4.5 fusion.5
  844.2 23.6 %while.1 = (s32[]{:T(128)}, f32[1024,1024]{1,0:T(8,128)}, s32[8,2]{0,1:T(2,128)S(1)}, f32[8,128,128]{2,1,0:T(8,128)S(1)}, s32[]{:T(128)}) while((s32[]{:T(128)}, f32[1024,1024]{1,0:T(8,128)}, s32[8,2]{0,1:T(2,128)S(1)}, f32[8,128,128]{2,1,0:T(8,128)S(1)}, s32[]{:T(128)}) %tuple.58), condition=%wide.while_cond, body=%wide.while_body.sunk | while | flops 2 | bytes 131189 | solution.py:55
  844.8 2.3 bitcast_dynamic-update-slice_fusion.2
  847.8 2.3 bitcast_dynamic-update-slice_fusion.2
  850.7 2.3 bitcast_dynamic-update-slice_fusion.2
  853.7 2.3 bitcast_dynamic-update-slice_fusion.2
  856.6 2.3 bitcast_dynamic-update-slice_fusion.2
  859.6 2.3 bitcast_dynamic-update-slice_fusion.2
  862.5 2.3 bitcast_dynamic-update-slice_fusion.2
  865.5 2.2 bitcast_dynamic-update-slice_fusion.2
  867.7 78.8 %custom-call.69 = f32[8,128,128]{1,2,0:T(8,128)S(1)} custom-call(f32[8,128,128]{2,1,0:T(8,128)S(1)} %get-tuple-element.12), custom_call_target="InvertDiagBlocksLowerTriangular" | custom-call | tf_op jit(solution)/shard_map/triangular_solve | solution.py:55
  947.1 1.9 convolution_subtract_fusion.5
  952.2 2.0 fusion.30
  954.9 2.2 fusion.33
  957.9 2.6 convolution_subtract_fusion.3
  961.2 2.8 convolution_subtract_fusion.2
  964.7 3.5 convolution_subtract_fusion.4
  971.2 52.9 %all-gather.11.cloned.1.call-done = f32[2048,1024]{1,0:T(8,128)} async-done(((f32[256,1024]{1,0:T(8,128)}), f32[2048,1024]{1,0:T(8,128)}) %all-gather.11.cloned.1.call-update) | async-done | bytes 8388624 | tf_op jit(solution)/shard_map/all_gather | solution.py:14
  1024.1 4.4 reduce_sum.45
  1028.7 16.7 %convolution_select_fusion = f32[2048,256]{1,0:T(8,128)} fusion(f32[2048,256]{1,0:T(8,128)S(1)} %bitcast.126, f32[2048,1024]{0,1:T(8,128)} %all-reduce.3.cloned.1.call-done, f32[256,1024]{1,0:T(8,128)S(1)} %reduce_sum.45, pred[2048]{0:T(1024)(128)(4,1)S(1)} %fusion.86), kind=kOutput, calls=%fused_computation.16 | convolution fusion | flops 6442975232 | bytes 13633536 | tf_op jit(solution)/shard_map/dot_general | solution.py:60
  (77 shorter events, 35.1 us)
Async XLA Ops:
  6.5 136.4 %all-gather.9.cloned.1.call-start = ((), (), s32[]{:S(2)}) async-start(), calls=%async_computation.2 | async-start | bytes 28311552 | tf_op jit(solution)/shard_map/all_gather | solution.py:14
  14.8 255.2 %all-gather.7.cloned.1.call-start = ((), (), s32[]{:S(2)}) async-start(), calls=%async_computation.1 | async-start | bytes 28311552 | tf_op jit(solution)/shard_map/all_gather | solution.py:14
  19.1 601.2 %all-reduce.3.cloned.1.call-start = ((), (), s32[]{:S(2)}) async-start(), calls=%async_computation | async-start | bytes 16777216 | tf_op jit(solution)/shard_map/psum | solution.py:51
  315.6 2.7 copy-start.2
  329.4 694.8 %all-gather.11.cloned.1.call-start = ((), (), s32[]{:S(2)}) async-start(), calls=%async_computation.3 | async-start | bytes 9437184 | tf_op jit(solution)/shard_map/all_gather | solution.py:14
  634.9 2.0 copy-start.1
  946.5 3.2 copy-start
Sparse Core Ops, SparseCore 0:
  14.9 127.9 all-gather.8
  144.8 125.1 all-gather.6
  329.5 290.8 all-reduce.2
  970.1 54.0 all-gather.10
